TPU v7x, 32 devices: a whole 2x2x4 slice. The times are simulated.
32 devices in a mesh: wide: 16 (over z, y, core), shift: 2 (over x).
Axes of the slice: x: 2, y: 2, z: 4, core: 2. Of those that a mesh axis runs over, the one named last changes fastest.
Arguments:
- particles: bfloat16 [1024, 8448], P('wide'), may hold values from -64 to 64
- group_id: int32 [1024, 1], P('wide'), may hold values from 0 to 15; in each aligned block of 64 rows (0 to 63, 64 to 127, ...) at most 8 rows name the same one
- ctf_curves: float32 [16, 4224], P('wide'), may hold values from -1 to 1
- projections: bfloat16 [16, 8448], P('wide')
- inv_noise: float32 [4224], replicated, may hold values from 0.5 to 2
- shifts: int32 [64, 2], P('shift'), may hold values from -8 to 8
Outputs:
- insertion: float32 [16, 12672], P('wide')
- log_evidence: float32 [1024], P('wide')
Inputs may be any that keep to these rules, and one draw needn't show every extreme that they name: `group_id`: at most 8 of the rows of one device name the same group, a bound that some block reaches.
All inputs are finite; a program needn't handle non-finite values.
Results may differ from a plain program's by a relative error of at most 0.0029.
Values may be sent and summed in bfloat16 or wider, within the bound.
A program may use at most 64 MiB of HBM per device.

v0:
```python
import math

import jax
import jax.numpy as jnp
from jax import lax
from jax.sharding import PartitionSpec as P

TWO_PI_BOX = 2.0 * math.pi / 128.0
HIGHEST_PRECISION = lax.Precision.HIGHEST


def shift_tables(shifts, coeffs):
    coeff_index = jnp.arange(coeffs, dtype=jnp.int32)
    freq_x = (coeff_index // 128).astype(jnp.float32)
    freq_y = (coeff_index % 128 - 64).astype(jnp.float32)
    move_x = shifts[:, 0].astype(jnp.float32)
    move_y = shifts[:, 1].astype(jnp.float32)
    phase_angle = TWO_PI_BOX * (
        move_x[:, None] * freq_x[None, :] + move_y[:, None] * freq_y[None, :]
    )
    return (jnp.cos(phase_angle), jnp.sin(phase_angle))


def rotate_slices(slab, cos_table, sin_table):
    coeffs = cos_table.shape[1]
    real_part = slab[:, :coeffs].astype(jnp.float32)[:, None, :]
    imag_part = slab[:, coeffs:].astype(jnp.float32)[:, None, :]
    rot_real = real_part * cos_table[None] + imag_part * sin_table[None]
    rot_imag = imag_part * cos_table[None] - real_part * sin_table[None]
    joined = jnp.concatenate([rot_real, rot_imag], 2)
    return joined.reshape(slab.shape[0] * cos_table.shape[0], 2 * coeffs).astype(jnp.bfloat16)


def slice_scores(weighted, weight_sq, slab, cos_table, sin_table):
    coeffs = cos_table.shape[1]
    n_trans = cos_table.shape[0]
    row_count = weighted.shape[0]
    rotated = rotate_slices(slab, cos_table, sin_table)
    cross_term = lax.dot_general(
        weighted, rotated, (((1,), (1,)), ((), ())), preferred_element_type=jnp.float32
    )
    slice_real = slab[:, :coeffs].astype(jnp.float32)
    slice_imag = slab[:, coeffs:].astype(jnp.float32)
    slice_power = slice_real * slice_real + slice_imag * slice_imag
    self_term = 0.5 * lax.dot_general(
        weight_sq, slice_power, (((1,), (1,)), ((), ())), precision=HIGHEST_PRECISION
    )
    scores = cross_term.reshape(row_count, slab.shape[0], n_trans) - self_term[:, :, None]
    return scores.reshape(row_count, slab.shape[0] * n_trans)


def local(particles, group_id, ctf_curves, projections, inv_noise, shifts):
    coeffs = inv_noise.shape[0]
    n_trans = shifts.shape[0]
    part_rows = particles.shape[0]
    cos_table, sin_table = shift_tables(shifts, coeffs)
    groups = group_id[:, 0]
    gathered_ctf = lax.all_gather(ctf_curves, "wide", axis=0, tiled=True)
    choose_group = (
        groups[:, None] == jnp.arange(gathered_ctf.shape[0], dtype=jnp.int32)[None, :]
    ).astype(jnp.float32)
    ctf_row = jnp.dot(choose_group, gathered_ctf, precision=HIGHEST_PRECISION)
    live_rows = jnp.ones((part_rows,), jnp.float32)
    row_count = particles.shape[0]
    real_part = particles[:, :coeffs].astype(jnp.float32)
    imag_part = particles[:, coeffs:].astype(jnp.float32)
    noise_ctf = inv_noise[None, :] * ctf_row
    weighted = jnp.concatenate([noise_ctf * real_part, noise_ctf * imag_part], 1).astype(
        jnp.bfloat16
    )
    filtered = jnp.concatenate([ctf_row * real_part, ctf_row * imag_part], 1).astype(jnp.bfloat16)
    weight_sq = ctf_row * ctf_row * inv_noise[None, :]
    ctf_square = ctf_row * ctf_row
    slab = lax.all_gather(projections, "wide", axis=0, tiled=True)
    amount = slab.shape[0]
    block_len = math.gcd(amount, 16)
    blocks = slab.reshape(amount // block_len, block_len, slab.shape[1])
    results = lax.map(
        lambda slab_block: slice_scores(weighted, weight_sq, slab_block, cos_table, sin_table),
        blocks,
    )
    scores = jnp.moveaxis(results, 0, 1).reshape(row_count, amount * n_trans)
    local_max = jnp.max(scores, 1)
    row_max = lax.pmax(local_max, "shift")
    row_total = lax.psum(jnp.sum(jnp.exp(scores - row_max[:, None]), 1), "shift")
    weights = (jnp.exp(scores - row_max[:, None]) / row_total[:, None]).astype(jnp.bfloat16)
    log_evidence = row_max + jnp.log(row_total)
    amount = projections.shape[0] * lax.axis_size("wide")
    block_len = math.gcd(amount, 16)

    def one_block(block_id):
        first_orient = block_id * block_len
        weight_block = lax.dynamic_slice_in_dim(
            weights, first_orient * n_trans, block_len * n_trans, 1
        )
        update = lax.dot_general(
            weight_block, filtered, (((0,), (0,)), ((), ())), preferred_element_type=jnp.float32
        )
        update = update.reshape(block_len, n_trans, 2 * coeffs)
        upd_real = update[:, :, :coeffs]
        upd_imag = update[:, :, coeffs:]
        data_real = jnp.sum(upd_real * cos_table[None] - upd_imag * sin_table[None], 1)
        data_imag = jnp.sum(upd_real * sin_table[None] + upd_imag * cos_table[None], 1)
        weight_sum = (
            jnp.sum(weight_block.astype(jnp.float32).reshape(row_count, block_len, n_trans), 2)
            * live_rows[:, None]
        )
        weight_data = lax.dot_general(
            weight_sum, ctf_square, (((0,), (0,)), ((), ())), precision=HIGHEST_PRECISION
        )
        return jnp.concatenate([data_real, data_imag, weight_data], 1)

    results = lax.map(one_block, jnp.arange(amount // block_len, dtype=jnp.int32))
    summed = lax.psum_scatter(
        results.reshape(amount, 3 * coeffs), "wide", scatter_dimension=0, tiled=True
    )
    insertion = lax.psum(summed, "shift")
    return (insertion, log_evidence)


def solution(mesh):
    placed = (
        P("wide", None),
        P("wide", None),
        P("wide", None),
        P("wide", None),
        P(),
        P("shift", None),
    )
    return jax.shard_map(
        local, mesh=mesh, in_specs=placed, out_specs=(P("wide", None), P("wide")), check_vma=False
    )
```

profile of v0, /device:TPU:0, one launch (start us, length us, event | category | flops | bytes accessed | tf_op | source)
XLA Modules:
  0.0 188.0 jit_solution(715756407361464335)
XLA Ops:
  7.2 0.0 copy-start
  7.2 0.0 all-reduce.3.cloned.1.call-start
  7.2 0.8 convert_bitcast_fusion.1
  8.0 24.1 %all-gather = f32[16,1,4224]{2,1,0:T(1,128)S(1)} all-gather(f32[1,1,4224]{2,1,0:T(1,128)} %bitcast.41), channel_id=1, replica_groups=mesh['wide'=16,'shift'=2] {'wide'}, dimensions={0}, use_global_device_ids=true | all-gather | bytes 287232 | tf_op jit(solution)/shard_map/all_gather | solution.py:58
  32.1 19.1 %all-gather.1 = bf16[16,1,8448]{2,1,0:T(2,128)(2,1)S(1)} all-gather(bf16[1,1,8448]{2,1,0:T(2,128)(2,1)} %bitcast.40), channel_id=1, replica_groups=mesh['wide'=16,'shift'=2] {'wide'}, dimensions={0}, use_global_device_ids=true | all-gather | bytes 287232 | tf_op jit(solution)/shard_map/all_gather | solution.py:74
  51.3 2.1 %fusion.8 = (bf16[64,4224]{1,0:T(8,128)(2,1)S(1)}, bf16[64,4224]{1,0:T(8,128)(2,1)S(1)}, bf16[64,4224]{1,0:T(8,128)(2,1)S(1)}, bf16[64,4224]{1,0:T(8,128)(2,1)S(1)}, f32[64,4224]{1,0:T(8,128)S(1)}) fusion(bf16[64,8448]{1,0:T(8,128)(2,1)} %param.6, f32[4224]{0:T(1024)} %param.10, f32[16,1,4224]{2,1,0:T(1,128)S(1)} %all-gather, s32[64]{0:T(128)} %bitcast.42), kind=kOutput, calls=%fused_computation.15 | convolution fusion | flops 54879232 | bytes 4612864 | tf_op jit(solution)/shard_map/dot_general | solution.py:62
  53.5 0.0 copy-done
  53.5 1.1 convolution_multiply_fusion
  54.6 2.0 %fusion.21 = (f32[32,4224]{1,0:T(8,128)S(1)}, f32[32,4224]{1,0:T(8,128)S(1)}) fusion(f32[4224]{0:T(1024)S(1)} %get-tuple-element.64, f32[32]{0:T(128)S(1)} %get-tuple-element.59, f32[4224]{0:T(1024)S(1)} %get-tuple-element.63, f32[32]{0:T(128)S(1)} %get-tuple-element.58), kind=kLoop, calls=%fused_computation.32 | loop fusion | flops 540672 | bytes 1115392 | tf_op jit(solution)/shard_map/cos | solution.py:21
  56.6 2.2 %add_convert_fusion = (bf16[16,32,4224]{2,1,0:T(8,128)(2,1)S(1)}, bf16[16,32,4224]{2,1,0:T(8,128)(2,1)S(1)}) fusion(f32[32,4224]{1,0:T(8,128)S(1)} %get-tuple-element.57, f32[16,4224]{1,0:T(8,128)S(1)} %get-tuple-element.48, f32[32,4224]{1,0:T(8,128)S(1)} %get-tuple-element.56, f32[16,4224]{1,0:T(8,128)S(1)} %get-tuple-element.47), kind=kLoop, calls=%fused_computation.7 | loop fusion | flops 17301504 | bytes 10272768 | tf_op jit(solution)/shard_map/convert.2
  58.7 2.4 %fusion.46 = (f32[64]{0:T(128)S(1)}, f32[64,16,32]{0,2,1:T(8,128)S(1)}) fusion(f32[64,16]{0,1:T(8,128)S(1)} %convolution_multiply_fusion, bf16[16,32,4224]{2,1,0:T(8,128)(2,1)S(1)} %get-tuple-element.46, bf16[16,32,4224]{2,1,0:T(8,128)(2,1)S(1)} %get-tuple-element.45, bf16[64,4224]{1,0:T(8,128)(2,1)S(1)} %get-tuple-element.43, ...), kind=kOutput, calls=%fused_computation.73 | convolution fusion | flops 573177792 | bytes 9867520 | tf_op jit(solution)/shard_map/while/body/eval_jaxpr/dot_general | solution.py:39
  61.1 4.9 %pmax.7 = f32[64]{0:T(128)S(1)} all-reduce(f32[64]{0:T(128)S(1)} %get-tuple-element.61), channel_id=1, replica_groups=mesh['wide'=16,'shift'=2] {'shift'}, use_global_device_ids=true, to_apply=%region_1.2 | all-reduce | flops 64 | bytes 512 | tf_op jit(solution)/shard_map/pmax | solution.py:84
  66.1 0.1 fusion.32
  66.2 5.1 %psum.14 = f32[64]{0:T(128)S(1)} all-reduce(f32[64]{0:T(128)S(1)} %fusion.32), channel_id=1, replica_groups=mesh['wide'=16,'shift'=2] {'shift'}, use_global_device_ids=true, to_apply=%region_3.4 | all-reduce | flops 64 | bytes 512 | tf_op jit(solution)/shard_map/psum | solution.py:85
  71.3 0.1 convert_reduce_fusion
  71.3 0.1 fusion.31
  71.4 0.7 fusion.17
  72.1 2.4 %fusion.13 = f32[16,32,8448]{2,1,0:T(8,128)S(1)} fusion(bf16[16,32,64]{2,1,0:T(8,128)(2,1)S(1)} %bitcast.39, bf16[64,4224]{1,0:T(8,128)(2,1)S(1)} %get-tuple-element.42, bf16[64,4224]{1,0:T(8,128)(2,1)S(1)} %get-tuple-element.34), kind=kOutput, calls=%fused_computation.22 | convolution fusion | flops 555810816 | bytes 18448384 | tf_op jit(solution)/shard_map/while/body/eval_jaxpr/dot_general | solution.py:96
  74.5 0.0 copy-start.1
  74.5 4.2 %subtract_reduce_fusion = (f32[16,4224]{1,0:T(8,128)S(1)}, f32[16,4224]{1,0:T(8,128)S(1)}) fusion(f32[16,32,8448]{2,1,0:T(8,128)S(1)} %fusion.13, f32[32,4224]{1,0:T(8,128)S(1)} %get-tuple-element.57, f32[32,4224]{1,0:T(8,128)S(1)} %get-tuple-element.56), kind=kLoop, calls=%fused_computation.5 | loop fusion | flops 17166336 | bytes 18923520 | tf_op jit(solution)/shard_map/while/body/eval_jaxpr/reduce_sum | solution.py:102
  78.7 1.0 pad_maximum_fusion
  79.6 0.0 all-reduce.3.cloned.1.call-update
  79.7 0.0 copy-done.1
  79.7 0.6 dynamic-slice.1
  80.3 0.5 log_add_fusion
  80.8 89.4 %all-reduce.3.cloned.1.call-done = f32[16,12672]{1,0:T(8,128)} async-done(((f32[16,12672]{1,0:T(8,128)}), f32[16,12672]{1,0:T(8,128)}) %all-reduce.3.cloned.1.call-update) | async-done | bytes 811024
  170.2 1.7 constant_dynamic-slice_fusion
  171.9 9.3 %psum.15 = f32[1,12672]{1,0:T(1,128)} all-reduce(f32[1,12672]{1,0:T(1,128)S(1)} %constant_dynamic-slice_fusion), channel_id=1, replica_groups=mesh['wide'=16,'shift'=2] {'shift'}, use_global_device_ids=true, to_apply=%region_8.9 | all-reduce | flops 12672 | bytes 101376 | tf_op jit(solution)/shard_map/psum | solution.py:117
  (3 shorter events, 0.1 us)
Async XLA Ops:
  7.2 46.3 %copy-start = (f32[4224]{0:T(1024)S(1)}, f32[4224]{0:T(1024)}, u32[]{:S(2)}) copy-start(f32[4224]{0:T(1024)} %param.10) | copy-start | bytes 50692
  7.2 163.0 %all-reduce.3.cloned.1.call-start = ((), (), s32[]{:S(2)}) async-start(), calls=%async_computation | async-start | bytes 1622016
  74.5 5.2 %copy-start.1 = (u32[32]{0:T(128)S(1)}, u32[32]{0:T(128)}, u32[]{:S(2)}) copy-start(u32[32]{0:T(128)} %constant.75) | copy-start | bytes 388
Sparse Core Ops, SparseCore 0:
  79.8 90.3 all-reduce.2
where the time goes:
time: 188 us
  waiting for transfers between devices  89.4 us (48%)
  blocking collectives  62.5 us (33%)
  between operations  14.1 us (8%)
  other arithmetic  10.9 us (6%)
  matrix products  8.68 us (5%)
  local copies, waits for them, and re-layouts  2.31 us (1%)
    unnamed x2, waiting for transfers between devices  89.4 us
    all_gather x1, blocking collectives, local(): gathered_ctf = lax.all_gather(ctf_curves, 'wide', axis=0, tiled=True)  24.1 us
    all_gather x1, blocking collectives, local(): slab = lax.all_gather(projections, 'wide', axis=0, tiled=True)  19.1 us
    psum x1, blocking collectives, local(): insertion = lax.psum(summed, 'shift')  9.26 us
    psum x1, blocking collectives, local(): lax.psum(jnp.sum(jnp.exp(scores - row_max[:, None]), 1), 'shift')  5.1 us
    pmax x1, blocking collectives, local(): row_max = lax.pmax(local_max, 'shift')  4.93 us
    reduce_sum x1, other arithmetic, one_block(): jnp.sum(upd_real * cos_table[None] - upd_imag * sin_table[None], 1)  4.2 us
  transfers between devices with their start and end apart: 1, of which 1 were waited for; matrix products, arithmetic and copies ran while one was open for 1% of the time, Pallas kernels for 0%

commit v1 on v0

v1 whole, which is shorter than its diff:
```python
import functools
import math

import jax
import jax.numpy as jnp
from jax import lax
from jax.experimental import pallas as pl
from jax.experimental.pallas import tpu as pltpu
from jax.sharding import PartitionSpec as P

LANE = 128
STEP = 2.0 * math.pi / 128.0
HIGH = lax.Precision.HIGHEST
MESH = pl.DeviceIdType.MESH
F32 = jnp.float32
BF16 = jnp.bfloat16
NT_DIMS = (((1,), (1,)), ((), ()))
NN_DIMS = (((1,), (0,)), ((), ()))


def dot(a, b, dims=NN_DIMS, precision=None):
    return lax.dot_general(a, b, dims, precision=precision, preferred_element_type=F32)


def kernel(
    cfg, x_hbm, gid_ref, ctf_ref, proj_ref, noise_ref, sh_ref,
    out_ref, ev_ref,
    xbuf, cbuf, pbuf, shbuf, cos_t, sin_t, wgt, fil, wsq, pf, power, selfc,
    sc, scr, tot, wts, wsum, part, r1, r2, fin, fbuf,
    x_sem, own_sem, ag_ssem, ag_rsem, rl_ssem, sh_ssem, sh_rsem,
    sc_ssem, sc_rsem, r1_ssem, r1_rsem, r2_ssem, r2_rsem, f_ssem, f_rsem,
):
    W, S, nl, L, NTL, R = cfg
    C = L * LANE
    NT = NTL * S
    H = W // 2
    NC = W // 2
    QB = 2
    NB = H // QB
    RB = QB * NT
    w = lax.axis_index("wide")
    s = lax.axis_index("shift")
    core = lax.rem(w, 2)
    chip = lax.div(w, 2)
    mate = chip * 2 + (1 - core)
    first = jnp.minimum(s * L, nl - L)
    start = pl.multiple_of(first * LANE, LANE)
    full = nl * LANE
    window = pl.ds(start, C)

    def chip_at(k):
        return lax.rem(chip + k, NC)

    def remote(src, dst, ssem, rsem, wide=None, shift=None):
        return pltpu.make_async_remote_copy(
            src_ref=src, dst_ref=dst, send_sem=ssem, recv_sem=rsem,
            device_id=(w if wide is None else wide, s if shift is None else shift),
            device_id_type=MESH,
        )

    x_copies = [
        pltpu.make_async_copy(
            x_hbm.at[:, pl.ds(pl.multiple_of(start + h * full, LANE), C)],
            xbuf.at[h], x_sem.at[h],
        )
        for h in range(2)
    ]
    own = [
        pltpu.make_async_copy(ctf_ref.at[:, window], cbuf.at[w], own_sem.at[0]),
        pltpu.make_async_copy(proj_ref.at[:, window], pbuf.at[w], own_sem.at[1]),
        pltpu.make_async_copy(sh_ref, shbuf.at[s], own_sem.at[2]),
    ]
    for c in own + x_copies:
        c.start()

    bar = pltpu.get_barrier_semaphore()
    pl.semaphore_signal(bar, inc=1, device_id=(mate, s), device_id_type=MESH)

    def greet(k, carry):
        pl.semaphore_signal(
            bar, inc=1, device_id=(chip_at(k) * 2 + core, s), device_id_type=MESH
        )
        return carry

    lax.fori_loop(1, NC, greet, 0)
    for d in range(1, S):
        pl.semaphore_signal(
            bar, inc=1, device_id=(w, lax.rem(s + d, S)), device_id_type=MESH
        )
    pl.semaphore_wait(bar, NC + S - 1)

    def ag_pair(k, to):
        return (
            remote(ctf_ref.at[:, window], cbuf.at[w], ag_ssem.at[0, k], ag_rsem.at[0, w], wide=to),
            remote(proj_ref.at[:, window], pbuf.at[w], ag_ssem.at[1, k], ag_rsem.at[1, w], wide=to),
        )

    def relay_pair(src):
        return (
            remote(cbuf.at[src], cbuf.at[src], rl_ssem.at[0, src], ag_rsem.at[0, src], wide=mate),
            remote(pbuf.at[src], pbuf.at[src], rl_ssem.at[1, src], ag_rsem.at[1, src], wide=mate),
        )

    sh_copies = [
        remote(sh_ref, shbuf.at[s], sh_ssem.at[d - 1], sh_rsem.at[s], shift=lax.rem(s + d, S))
        for d in range(1, S)
    ]
    for c in sh_copies:
        c.start()

    def ag_start(k, carry):
        for c in ag_pair(k, chip_at(k) * 2 + core):
            c.start()
        return carry

    lax.fori_loop(1, NC, ag_start, 0)
    for c in ag_pair(0, mate):
        c.start()

    for c in own:
        c.wait()
    for d in range(1, S):
        other = lax.rem(s + d, S)
        remote(sh_ref, shbuf.at[other], sh_ssem.at[d - 1], sh_rsem.at[other], shift=other).wait_recv()

    sh = shbuf[...].reshape(NT, LANE)
    lane = lax.broadcasted_iota(jnp.int32, (NT, LANE), 1)
    ang_b = STEP * (sh[:, 1:2] * (lane - 64).astype(F32))
    kx = first + lane
    ang_a = STEP * (sh[:, 0:1] * kx.astype(F32))
    live = jnp.where(kx >= s * L, 1.0, 0.0)
    cos_b, sin_b = jnp.cos(ang_b), jnp.sin(ang_b)
    cos_a, sin_a = jnp.cos(ang_a) * live, jnp.sin(ang_a) * live
    for l in range(L):
        ca, sa = cos_a[:, l : l + 1], sin_a[:, l : l + 1]
        cols = pl.ds(l * LANE, LANE)
        cos_t[:, cols] = ca * cos_b - sa * sin_b
        sin_t[:, cols] = sa * cos_b + ca * sin_b

    def relay(k, carry):
        src = lax.rem(chip + NC - k, NC) * 2 + core
        for c in relay_pair(src):
            c.wait_recv()
            c.start()
        return carry

    lax.fori_loop(1, NC, relay, 0)

    def landed(j, carry):
        for c in relay_pair(j * 2 + (1 - core)):
            c.wait_recv()
        return carry

    lax.fori_loop(0, NC, landed, 0)
    for c in x_copies:
        c.wait()

    onehot = jnp.where(
        gid_ref[...] == lax.broadcasted_iota(jnp.int32, (R, part.shape[2] - C), 1), 1.0, 0.0
    )
    pick = onehot[:, :W]
    for l in range(L):
        cols = pl.ds(l * LANE, LANE)
        curves = cbuf[:, 0, cols]
        row = dot(pick, curves, precision=HIGH)
        noise = noise_ref[:, pl.ds(pl.multiple_of(start + l * LANE, LANE), LANE)]
        x_re = xbuf[0, :, cols].astype(F32)
        x_im = xbuf[1, :, cols].astype(F32)
        gain = noise * row
        re, im = pl.ds(2 * l * LANE, LANE), pl.ds((2 * l + 1) * LANE, LANE)
        wgt[:, re] = (gain * x_re).astype(BF16)
        wgt[:, im] = (gain * x_im).astype(BF16)
        fil[:, re] = (row * x_re).astype(BF16)
        fil[:, im] = (row * x_im).astype(BF16)
        here = jnp.where(first + l >= s * L, 0.5, 0.0)
        wsq[:, cols] = curves * curves * noise * here

    def widen(o, carry):
        p = pbuf[o].astype(F32)
        pf[o] = p
        power[pl.ds(o, 1), :] = jnp.sum(p * p, axis=0, keepdims=True)
        return carry

    lax.fori_loop(0, W, widen, 0)
    self_g = dot(power[...], wsq[...], NT_DIMS, HIGH)
    self_i = dot(self_g, pick, NT_DIMS, HIGH)
    selfc[...] = jnp.concatenate([self_i[:H], self_i[H:]], axis=1)

    def sc_copy(b, d):
        rows = pl.ds(pl.multiple_of(b * RB, RB), RB)
        return remote(
            sc.at[rows], scr.at[d - 1, rows], sc_ssem.at[d - 1, b], sc_rsem.at[d - 1, b],
            shift=lax.rem(s + d, S),
        )

    def score_block(b, carry):
        acc = jnp.zeros((2 * RB, R), F32)
        for l in range(L):
            cols = pl.ds(l * LANE, LANE)
            ct, st = cos_t[:, cols], sin_t[:, cols]
            rots = []
            for h in range(2):
                for q in range(QB):
                    o = h * H + b * QB + q
                    pr = pf[o, 0:1, cols]
                    pi = pf[o, 1:2, cols]
                    rots.append(
                        jnp.concatenate(
                            [(pr * ct + pi * st).astype(BF16), (pi * ct - pr * st).astype(BF16)],
                            axis=1,
                        )
                    )
            rot = jnp.concatenate(rots, axis=0)
            acc = acc + dot(rot, wgt[:, pl.ds(2 * l * LANE, 2 * LANE)], NT_DIMS)
        both = jnp.concatenate([acc[:RB], acc[RB:]], axis=1)
        for q in range(QB):
            rows = pl.ds(pl.multiple_of(b * RB + q * NT, NT), NT)
            sc[rows, :] = both[q * NT : (q + 1) * NT] - selfc[pl.ds(b * QB + q, 1), :]
        for d in range(1, S):
            sc_copy(b, d).start()
        return carry

    lax.fori_loop(0, NB, score_block, 0)

    def swap(v):
        return pltpu.roll(v, R, 1)

    def join(b, m):
        rows = pl.ds(pl.multiple_of(b * RB, RB), RB)
        v = sc[rows, :]
        for d in range(1, S):
            sc_copy(b, d).wait_recv()
            v = v + scr[d - 1, rows, :]
        tot[rows, :] = v
        return jnp.maximum(m, jnp.max(v.reshape(RB // 8, 8, 2 * R), axis=0))

    m8 = lax.fori_loop(0, NB, join, jnp.full((8, 2 * R), -jnp.inf, F32))
    top = jnp.max(m8, axis=0, keepdims=True)
    top = jnp.maximum(top, swap(top))

    def expo(b, t):
        rows = pl.ds(pl.multiple_of(b * RB, RB), RB)
        e = jnp.exp(tot[rows, :] - top)
        tot[rows, :] = e
        return t + jnp.sum(e.reshape(RB // 8, 8, 2 * R), axis=0)

    t8 = lax.fori_loop(0, NB, expo, jnp.zeros((8, 2 * R), F32))
    total = jnp.sum(t8, axis=0, keepdims=True)
    total = total + swap(total)
    ev_ref[...] = (top + jnp.log(total))[:, :R]

    def norm(o, carry):
        rows = pl.ds(pl.multiple_of(o * NT, NT), NT)
        v = (tot[rows, :] / total).astype(BF16)
        wts[0, rows, :] = v[:, :R]
        wts[1, rows, :] = v[:, R:]
        wsum[pl.ds(o, 1), :] = jnp.sum(v.astype(F32), axis=0, keepdims=True)
        return carry

    lax.fori_loop(0, H, norm, 0)

    loads = wsum[...]
    extra = pl.ds(C, part.shape[2] - C)
    for h in range(2):
        load = dot(loads[:, h * R : (h + 1) * R], onehot, precision=HIGH)
        for o in range(H):
            part[h * H + o, 0:1, extra] = load[o : o + 1]
            part[h * H + o, 1:2, extra] = jnp.zeros_like(load[o : o + 1])

    def update_line(l, carry):
        cols = pl.ds(pl.multiple_of(l * LANE, LANE), LANE)
        ct, st = cos_t[:, cols], sin_t[:, cols]
        data = fil[:, pl.ds(pl.multiple_of(l * 2 * LANE, LANE), 2 * LANE)]
        for h in range(2):
            for o in range(0, H, 4):
                u = dot(wts[h, o * NT : (o + 4) * NT, :], data)
                for q in range(4):
                    ur = u[q * NT : (q + 1) * NT, :LANE]
                    ui = u[q * NT : (q + 1) * NT, LANE:]
                    at = h * H + o + q
                    part[at, 0:1, cols] = jnp.sum(ur * ct - ui * st, axis=0, keepdims=True)
                    part[at, 1:2, cols] = jnp.sum(ur * st + ui * ct, axis=0, keepdims=True)
        return carry

    lax.fori_loop(0, L, update_line, 0)

    def r1_copy(j):
        return remote(part.at[2 * j + (1 - core)], r1.at[j], r1_ssem.at[j], r1_rsem.at[j], wide=mate)

    def r2_copy(k):
        to = chip_at(k)
        return remote(
            part.at[2 * to + core], r2.at[k], r2_ssem.at[k], r2_rsem.at[k], wide=2 * to + core
        )

    def r1_start(k, carry):
        r1_copy(chip_at(k)).start()
        return carry

    lax.fori_loop(1, NC, r1_start, 0)
    r1_copy(chip).start()

    def r1_take(k, carry):
        j = chip_at(k)
        r1_copy(j).wait_recv()
        part[2 * j + core] = part[2 * j + core] + r1[j]
        r2_copy(k).start()
        return carry

    lax.fori_loop(1, NC, r1_take, 0)
    r1_copy(chip).wait_recv()
    fin[...] = part[w] + r1[chip]

    def r2_take(k, carry):
        r2_copy(k).wait_recv()
        fin[...] = fin[...] + r2[k]
        return carry

    lax.fori_loop(1, NC, r2_take, 0)

    load = fin[0:1, C : C + W]
    curves = cbuf[:, 0, :]
    fbuf[s, 0:2, :] = fin[:, :C]
    fbuf[s, 2:3, :] = dot(load, curves * curves, precision=HIGH)

    def f_copy(d):
        return remote(
            fbuf.at[s], fbuf.at[s], f_ssem.at[d - 1], f_rsem.at[s], shift=lax.rem(s + d, S)
        )

    for d in range(1, S):
        f_copy(d).start()
    for d in range(1, S):
        other = lax.rem(s + d, S)
        remote(fbuf.at[other], fbuf.at[other], f_ssem.at[d - 1], f_rsem.at[other], shift=other).wait_recv()
    for t in range(S):
        lo, hi = t * L, min(t * L + L, nl)
        if lo < hi:
            off = lo - min(lo, nl - L)
            for r in range(3):
                out_ref[r : r + 1, lo * LANE : hi * LANE] = fbuf[
                    t, r : r + 1, off * LANE : (off + hi - lo) * LANE
                ]

    for c in sh_copies:
        c.wait_send()
    for c in ag_pair(0, mate):
        c.wait_send()
    r1_copy(chip).wait_send()

    def drain(k, carry):
        for c in ag_pair(k, chip_at(k) * 2 + core):
            c.wait_send()
        for c in relay_pair(lax.rem(chip + NC - k, NC) * 2 + core):
            c.wait_send()
        r1_copy(chip_at(k)).wait_send()
        r2_copy(k).wait_send()
        return carry

    lax.fori_loop(1, NC, drain, 0)

    def drain_sc(b, carry):
        for d in range(1, S):
            sc_copy(b, d).wait_send()
        return carry

    lax.fori_loop(0, NB, drain_sc, 0)
    for d in range(1, S):
        f_copy(d).wait_send()


def local(W, S, particles, group_id, ctf_curves, projections, inv_noise, shifts):
    R = particles.shape[0]
    coeffs = inv_noise.shape[0]
    nl = coeffs // LANE
    L = -(-nl // S)
    C = L * LANE
    NTL = shifts.shape[0]
    NT = NTL * S
    H = W // 2
    NB = H // 2
    G = -(-W // LANE) * LANE
    rows = H * NT
    any_spec = pl.BlockSpec(memory_space=pl.ANY)
    vm = pl.BlockSpec(memory_space=pltpu.VMEM)
    dma = pltpu.SemaphoreType.DMA
    sh = jnp.pad(shifts.astype(F32), ((0, 0), (0, LANE - shifts.shape[1])))
    V = pltpu.VMEM
    out, ev = pl.pallas_call(
        functools.partial(kernel, (W, S, nl, L, NTL, R)),
        out_shape=(
            jax.ShapeDtypeStruct((3, coeffs), F32),
            jax.ShapeDtypeStruct((1, R), F32),
        ),
        in_specs=[any_spec, vm, vm, vm, vm, vm],
        out_specs=(vm, vm),
        scratch_shapes=[
            V((2, R, C), BF16),
            V((W, 1, C), F32),
            V((W, 2, C), BF16),
            V((S, NTL, LANE), F32),
            V((NT, C), F32),
            V((NT, C), F32),
            V((R, 2 * C), BF16),
            V((R, 2 * C), BF16),
            V((W, C), F32),
            V((W, 2, C), F32),
            V((W, C), F32),
            V((H, 2 * R), F32),
            V((rows, 2 * R), F32),
            V((max(S - 1, 1), rows, 2 * R), F32),
            V((rows, 2 * R), F32),
            V((2, rows, R), BF16),
            V((H, 2 * R), F32),
            V((W, 2, C + G), F32),
            V((W // 2, 2, C + G), F32),
            V((W // 2, 2, C + G), F32),
            V((2, C + G), F32),
            V((S, 4, C), F32),
            dma((2,)), dma((3,)),
            dma((2, W // 2)), dma((2, W)), dma((2, W)),
            dma((S,)), dma((S,)),
            dma((S, NB)), dma((S, NB)),
            dma((W // 2,)), dma((W // 2,)),
            dma((W // 2,)), dma((W // 2,)),
            dma((S,)), dma((S,)),
        ],
        compiler_params=pltpu.CompilerParams(
            collective_id=0, has_side_effects=True, vmem_limit_bytes=60 * 1024 * 1024
        ),
    )(
        particles, group_id, ctf_curves, projections.reshape(2, coeffs),
        inv_noise.reshape(1, coeffs), sh,
    )
    return out.reshape(1, 3 * coeffs), ev.reshape(R)


def solution(mesh):
    W, S = mesh.shape["wide"], mesh.shape["shift"]
    placed = (
        P("wide", None),
        P("wide", None),
        P("wide", None),
        P("wide", None),
        P(),
        P("shift", None),
    )
    return jax.shard_map(
        functools.partial(local, W, S), mesh=mesh, in_specs=placed,
        out_specs=(P("wide", None), P("wide")), check_vma=False,
    )
```

time: 188 us -> 48.9 us (0.26)
  waiting for transfers between devices: 89.4 us -> 0 us
  blocking collectives: 62.5 us -> 0 us
  Pallas kernels: 0 us -> 39.6 us
  between operations: 14.1 us -> 0.64 us
  other arithmetic: 10.9 us -> 1.54 us
  matrix products: 8.68 us -> 0 us
  local copies, waits for them, and re-layouts: 2.31 us -> 6.73 us
    unnamed x2 -> x0, waiting for transfers between devices: 89.4 us -> none
    all_gather x2 -> x0, blocking collectives: 43.2 us -> none  [the longest x1 24.1 us: local(): gathered_ctf = lax.all_gather(ctf_curves, 'wide', axis=0, tiled=True)]
    pallas_call x0 -> x1, Pallas kernels: none -> 39.6 us  [local(): pl.pallas_call(functools.partial(kernel, (W, S, nl, L, NTL, R)), out_shap...]
    psum x2 -> x0, blocking collectives: 14.4 us -> none  [the longest x1 9.26 us: local(): insertion = lax.psum(summed, 'shift')]
    dot_general x5 -> x0, matrix products: 8.68 us -> none  [the longest x1 2.4 us: one_block(): lax.dot_general(weight_block, filtered, (((0,), (0,)), ((), ())), preferr...]
    pmax x1 -> x0, blocking collectives: 4.93 us -> none  [local(): row_max = lax.pmax(local_max, 'shift')]
    reduce_sum x3 -> x0, other arithmetic: 4.37 us -> none  [the longest x1 4.2 us: one_block(): jnp.sum(upd_real * cos_table[None] - upd_imag * sin_table[None], 1)]
    another operation x1 -> x0, other arithmetic: 2.17 us -> none
  transfers between devices with their start and end apart: 1 -> 0, of which waited for: 1 -> 0; matrix products, arithmetic and copies ran while one was open for 1% -> 0% of each run, Pallas kernels for 0% -> 0%
where the time goes in v1:
time: 48.9 us; the launch traced here: 48.5 us
  Pallas kernels  39.6 us (81%)
  local copies, waits for them, and re-layouts  6.73 us (14%)
  other arithmetic  1.54 us (3%)
  between operations  0.64 us (1%)
    pallas_call x1, Pallas kernels, local(): pl.pallas_call(functools.partial(kernel, (W, S, nl, L, NTL, R)), out_shap...  39.6 us
    unnamed x3, local copies, waits for them, and re-layouts  4.08 us
    reshape x1, local copies, waits for them, and re-layouts, local(): inv_noise.reshape(1, coeffs)  1.34 us

profile of v1, /device:TPU:0, one launch (start us, length us, event | category | flops | bytes accessed | tf_op | source)
XLA Modules:
  0.0 48.5 jit_solution(10752495853477504588)
XLA Ops:
  0.6 0.7 %convert_element_type.5 = f32[32,2]{0,1:T(2,128)S(1)} convert(s32[32,2]{0,1:T(2,128)} %param.11) | non-fusion elementwise | flops 64 | bytes 512 | tf_op jit(solution)/shard_map/convert_element_type | solution.py:387
  1.3 0.1 copy.10
  1.4 0.6 %pad.4.sh_ref = f32[32,128]{1,0:T(8,128)} pad(f32[32,2]{1,0:T(8,128)S(1)} %copy.10, f32[]{:T(128)} %constant.2.clone.1), padding=0_0x0_126 | pad | bytes 16644 | tf_op jit(solution)/shard_map/jit(_pad)/pad | solution.py:387
  2.0 1.3 %reshape.17.noise_ref = f32[1,4224]{1,0:T(1,128)} reshape(f32[4224]{0:T(1024)} %param.10) | data formatting | bytes 33792 | tf_op jit(solution)/shard_map/reshape | solution.py:433
  3.3 0.9 %reduce = bf16[8448]{0:T(1024)(128)(2,1)S(1)} reduce(bf16[1,8448]{1,0:T(2,128)(2,1)} %param.9, bf16[]{:T(256)} %constant.7), dimensions={0}, to_apply=%param.9.reduce_sub_computation | reduce | bytes 33794 | tf_op args[3]
  4.2 0.6 %reshape.16.proj_ref = bf16[2,4224]{1,0:T(2,128)(2,1)} reshape(bf16[8448]{0:T(1024)(128)(2,1)S(1)} %reduce) | data formatting | bytes 33792 | tf_op jit(solution)/shard_map/reshape | solution.py:432
  4.8 1.4 %copy.11.gid_ref = s32[64,1]{1,0:T(8,128)} copy(s32[64,1]{0,1:T(1,128)} %param.7) | data formatting | bytes 512 | tf_op args[1]
  6.2 39.6 %shard_map.77 = (f32[3,4224]{1,0:T(4,128)}, f32[1,64]{1,0:T(1,128)}) custom-call(bf16[64,8448]{1,0:T(8,128)(2,1)} %x_hbm.1, s32[64,1]{1,0:T(8,128)} %copy.11.gid_ref, f32[1,4224]{1,0:T(1,128)} %ctf_ref.1, bf16[2,4224]{1,0:T(2,128)(2,1)} %reshape.16.proj_ref, f32[1,4224]{1,0:T(1,128)} %reshape.17.noise_ref, f32[32,128]{1,0:T(8,128)} %pad.4.sh_ref), custom_call_target="tpu_custom_call" | custom-call | tf_op jit(solution)/shard_map/pallas_call | solution.py:389
  45.8 1.6 %copy.12 = f32[1,1,3,4224]{3,1,2,0:T(1,128)} copy(f32[1,1,3,4224]{3,2,1,0:T(4,128)} %bitcast.4) | data formatting | bytes 101376
  47.4 1.2 %copy.14 = f32[64]{0:T(128)} copy(f32[64]{0:T(128)} %bitcast.6) | data formatting | bytes 512

commit v2 on v1

--- a/solution.py
+++ b/solution.py
@@ -16,6 +16,7 @@
 BF16 = jnp.bfloat16
 NT_DIMS = (((1,), (1,)), ((), ()))
 NN_DIMS = (((1,), (0,)), ((), ()))
+TN_DIMS = (((0,), (0,)), ((), ()))
 
 
 def dot(a, b, dims=NN_DIMS, precision=None):
@@ -25,7 +26,7 @@
 def kernel(
     cfg, x_hbm, gid_ref, ctf_ref, proj_ref, noise_ref, sh_ref,
     out_ref, ev_ref,
-    xbuf, cbuf, pbuf, shbuf, cos_t, sin_t, wgt, fil, wsq, pf, power, selfc,
+    xbuf, cbuf, pbuf, shbuf, prow, nbuf, cos_t, sin_t, wgt, fil, wsq, pf, power, selfc,
     sc, scr, tot, wts, wsum, part, r1, r2, fin, fbuf,
     x_sem, own_sem, ag_ssem, ag_rsem, rl_ssem, sh_ssem, sh_rsem,
     sc_ssem, sc_rsem, r1_ssem, r1_rsem, r2_ssem, r2_rsem, f_ssem, f_rsem,
@@ -67,11 +68,16 @@
     ]
     own = [
         pltpu.make_async_copy(ctf_ref.at[:, window], cbuf.at[w], own_sem.at[0]),
-        pltpu.make_async_copy(proj_ref.at[:, window], pbuf.at[w], own_sem.at[1]),
+        pltpu.make_async_copy(proj_ref, prow, own_sem.at[1]),
         pltpu.make_async_copy(sh_ref, shbuf.at[s], own_sem.at[2]),
+        pltpu.make_async_copy(noise_ref, nbuf.at[0], own_sem.at[3]),
     ]
     for c in own + x_copies:
         c.start()
+
+    own[1].wait()
+    for h in range(2):
+        pbuf[w, h : h + 1, :] = prow[:, pl.ds(pl.multiple_of(start + h * full, LANE), C)]
 
     bar = pltpu.get_barrier_semaphore()
     pl.semaphore_signal(bar, inc=1, device_id=(mate, s), device_id_type=MESH)
@@ -92,7 +98,7 @@
     def ag_pair(k, to):
         return (
             remote(ctf_ref.at[:, window], cbuf.at[w], ag_ssem.at[0, k], ag_rsem.at[0, w], wide=to),
-            remote(proj_ref.at[:, window], pbuf.at[w], ag_ssem.at[1, k], ag_rsem.at[1, w], wide=to),
+            remote(pbuf.at[w], pbuf.at[w], ag_ssem.at[1, k], ag_rsem.at[1, w], wide=to),
         )
 
     def relay_pair(src):
@@ -117,17 +123,22 @@
     for c in ag_pair(0, mate):
         c.start()
 
-    for c in own:
+    for c in own[:1] + own[2:]:
         c.wait()
     for d in range(1, S):
         other = lax.rem(s + d, S)
         remote(sh_ref, shbuf.at[other], sh_ssem.at[d - 1], sh_rsem.at[other], shift=other).wait_recv()
 
-    sh = shbuf[...].reshape(NT, LANE)
-    lane = lax.broadcasted_iota(jnp.int32, (NT, LANE), 1)
-    ang_b = STEP * (sh[:, 1:2] * (lane - 64).astype(F32))
-    kx = first + lane
-    ang_a = STEP * (sh[:, 0:1] * kx.astype(F32))
+    lane = lax.broadcasted_iota(jnp.int32, (2, 2 * LANE), 1)
+    axis = lax.broadcasted_iota(jnp.int32, (2, 2 * LANE), 0)
+    freq = jnp.where(
+        lane < LANE, jnp.where(axis == 0, first + lane, 0), jnp.where(axis == 1, lane - LANE - 64, 0)
+    ).astype(F32)
+    ang = STEP * jnp.concatenate(
+        [dot(shbuf[t].astype(F32), freq, TN_DIMS, HIGH) for t in range(S)], axis=0
+    )
+    ang_a, ang_b = ang[:, :LANE], ang[:, LANE:]
+    kx = first + lax.broadcasted_iota(jnp.int32, (NT, LANE), 1)
     live = jnp.where(kx >= s * L, 1.0, 0.0)
     cos_b, sin_b = jnp.cos(ang_b), jnp.sin(ang_b)
     cos_a, sin_a = jnp.cos(ang_a) * live, jnp.sin(ang_a) * live
@@ -156,14 +167,14 @@
         c.wait()
 
     onehot = jnp.where(
-        gid_ref[...] == lax.broadcasted_iota(jnp.int32, (R, part.shape[2] - C), 1), 1.0, 0.0
+        gid_ref[...] == lax.broadcasted_iota(jnp.int32, (part.shape[2] - C, R), 0), 1.0, 0.0
     )
-    pick = onehot[:, :W]
+    pick = onehot[:W]
     for l in range(L):
         cols = pl.ds(l * LANE, LANE)
         curves = cbuf[:, 0, cols]
-        row = dot(pick, curves, precision=HIGH)
-        noise = noise_ref[:, pl.ds(pl.multiple_of(start + l * LANE, LANE), LANE)]
+        row = dot(pick, curves, TN_DIMS, HIGH)
+        noise = nbuf[:, pl.ds(pl.multiple_of(start + l * LANE, LANE), LANE)]
         x_re = xbuf[0, :, cols].astype(F32)
         x_im = xbuf[1, :, cols].astype(F32)
         gain = noise * row
@@ -183,7 +194,7 @@
 
     lax.fori_loop(0, W, widen, 0)
     self_g = dot(power[...], wsq[...], NT_DIMS, HIGH)
-    self_i = dot(self_g, pick, NT_DIMS, HIGH)
+    self_i = dot(self_g, pick, NN_DIMS, HIGH)
     selfc[...] = jnp.concatenate([self_i[:H], self_i[H:]], axis=1)
 
     def sc_copy(b, d):
@@ -262,27 +273,10 @@
     loads = wsum[...]
     extra = pl.ds(C, part.shape[2] - C)
     for h in range(2):
-        load = dot(loads[:, h * R : (h + 1) * R], onehot, precision=HIGH)
+        load = dot(loads[:, h * R : (h + 1) * R], onehot, NT_DIMS, HIGH)
         for o in range(H):
             part[h * H + o, 0:1, extra] = load[o : o + 1]
             part[h * H + o, 1:2, extra] = jnp.zeros_like(load[o : o + 1])
-
-    def update_line(l, carry):
-        cols = pl.ds(pl.multiple_of(l * LANE, LANE), LANE)
-        ct, st = cos_t[:, cols], sin_t[:, cols]
-        data = fil[:, pl.ds(pl.multiple_of(l * 2 * LANE, LANE), 2 * LANE)]
-        for h in range(2):
-            for o in range(0, H, 4):
-                u = dot(wts[h, o * NT : (o + 4) * NT, :], data)
-                for q in range(4):
-                    ur = u[q * NT : (q + 1) * NT, :LANE]
-                    ui = u[q * NT : (q + 1) * NT, LANE:]
-                    at = h * H + o + q
-                    part[at, 0:1, cols] = jnp.sum(ur * ct - ui * st, axis=0, keepdims=True)
-                    part[at, 1:2, cols] = jnp.sum(ur * st + ui * ct, axis=0, keepdims=True)
-        return carry
-
-    lax.fori_loop(0, L, update_line, 0)
 
     def r1_copy(j):
         return remote(part.at[2 * j + (1 - core)], r1.at[j], r1_ssem.at[j], r1_rsem.at[j], wide=mate)
@@ -293,21 +287,38 @@
             part.at[2 * to + core], r2.at[k], r2_ssem.at[k], r2_rsem.at[k], wide=2 * to + core
         )
 
-    def r1_start(k, carry):
-        r1_copy(chip_at(k)).start()
-        return carry
-
-    lax.fori_loop(1, NC, r1_start, 0)
-    r1_copy(chip).start()
-
-    def r1_take(k, carry):
+    def update_chip(j):
+        h = lax.div(2 * j, H)
+        rows = pl.ds(pl.multiple_of(lax.rem(2 * j, H) * NT, 2 * NT), 2 * NT)
+        pair = wts[h, rows, :]
+        for l in range(L):
+            cols = pl.ds(l * LANE, LANE)
+            ct, st = cos_t[:, cols], sin_t[:, cols]
+            u = dot(pair, fil[:, pl.ds(2 * l * LANE, 2 * LANE)])
+            for q in range(2):
+                ur = u[q * NT : (q + 1) * NT, :LANE]
+                ui = u[q * NT : (q + 1) * NT, LANE:]
+                part[2 * j + q, 0:1, cols] = jnp.sum(ur * ct - ui * st, axis=0, keepdims=True)
+                part[2 * j + q, 1:2, cols] = jnp.sum(ur * st + ui * ct, axis=0, keepdims=True)
+
+    def r1_take(k):
         j = chip_at(k)
         r1_copy(j).wait_recv()
         part[2 * j + core] = part[2 * j + core] + r1[j]
         r2_copy(k).start()
-        return carry
-
-    lax.fori_loop(1, NC, r1_take, 0)
+
+    def update_step(k, carry):
+        j = chip_at(k)
+        update_chip(j)
+        r1_copy(j).start()
+
+        @pl.when(jnp.logical_and(k >= 2, k <= NC))
+        def _():
+            r1_take(k - 1)
+
+        return carry
+
+    lax.fori_loop(1, NC + 1, update_step, 0)
     r1_copy(chip).wait_recv()
     fin[...] = part[w] + r1[chip]
 
@@ -367,6 +378,13 @@
     lax.fori_loop(0, NB, drain_sc, 0)
     for d in range(1, S):
         f_copy(d).wait_send()
+
+
+def unfold(rows_ref, ev_in, out_ref, ev_ref):
+    n = rows_ref.shape[1]
+    for r in range(3):
+        out_ref[:, r * n : (r + 1) * n] = rows_ref[r : r + 1, :]
+    ev_ref[...] = ev_in[...]
 
 
 def local(W, S, particles, group_id, ctf_curves, projections, inv_noise, shifts):
@@ -384,7 +402,6 @@
     any_spec = pl.BlockSpec(memory_space=pl.ANY)
     vm = pl.BlockSpec(memory_space=pltpu.VMEM)
     dma = pltpu.SemaphoreType.DMA
-    sh = jnp.pad(shifts.astype(F32), ((0, 0), (0, LANE - shifts.shape[1])))
     V = pltpu.VMEM
     out, ev = pl.pallas_call(
         functools.partial(kernel, (W, S, nl, L, NTL, R)),
@@ -392,13 +409,15 @@
             jax.ShapeDtypeStruct((3, coeffs), F32),
             jax.ShapeDtypeStruct((1, R), F32),
         ),
-        in_specs=[any_spec, vm, vm, vm, vm, vm],
+        in_specs=[any_spec, vm, any_spec, any_spec, any_spec, any_spec],
         out_specs=(vm, vm),
         scratch_shapes=[
             V((2, R, C), BF16),
             V((W, 1, C), F32),
             V((W, 2, C), BF16),
-            V((S, NTL, LANE), F32),
+            V((S, 2, NTL), jnp.int32),
+            V((1, 2 * coeffs), BF16),
+            V((1, coeffs), F32),
             V((NT, C), F32),
             V((NT, C), F32),
             V((R, 2 * C), BF16),
@@ -417,7 +436,7 @@
             V((W // 2, 2, C + G), F32),
             V((2, C + G), F32),
             V((S, 4, C), F32),
-            dma((2,)), dma((3,)),
+            dma((2,)), dma((4,)),
             dma((2, W // 2)), dma((2, W)), dma((2, W)),
             dma((S,)), dma((S,)),
             dma((S, NB)), dma((S, NB)),
@@ -429,10 +448,18 @@
             collective_id=0, has_side_effects=True, vmem_limit_bytes=60 * 1024 * 1024
         ),
     )(
-        particles, group_id, ctf_curves, projections.reshape(2, coeffs),
-        inv_noise.reshape(1, coeffs), sh,
+        particles, group_id.reshape(1, R), ctf_curves, projections, inv_noise, shifts.T,
     )
-    return out.reshape(1, 3 * coeffs), ev.reshape(R)
+    out, ev = pl.pallas_call(
+        unfold,
+        out_shape=(
+            jax.ShapeDtypeStruct((1, 3 * coeffs), F32),
+            jax.ShapeDtypeStruct((1, R), F32),
+        ),
+        in_specs=[vm, vm],
+        out_specs=(vm, vm),
+    )(out, ev)
+    return out, ev.reshape(R)
 
 
 def solution(mesh):

time: 48.9 us -> 39.7 us (0.81)
  local copies, waits for them, and re-layouts: 6.73 us -> 0 us
  other arithmetic: 1.54 us -> 0 us
  Pallas kernels: 39.6 us -> 38.9 us
    unnamed x3 -> x0, local copies, waits for them, and re-layouts: 4.08 us -> none
    pallas_call x1, Pallas kernels: 39.6 us -> 37.4 us  [local(): pl.pallas_call(functools.partial(kernel, (W, S, nl, L, NTL, R)), out_shap...]
    reshape x2 -> x0, local copies, waits for them, and re-layouts: 1.96 us -> none  [the longest x1 1.34 us: local(): inv_noise.reshape(1, coeffs)]
    pallas_call x0 -> x1, Pallas kernels: none -> 1.52 us  [local(): pl.pallas_call(unfold, out_shape=(jax.ShapeDtypeStruct((1, 3 * coeffs), F...]
    unnamed x1 -> x0, other arithmetic: 0.86 us -> none
    convert_element_type x1 -> x0, other arithmetic: 0.68 us -> none  [local(): sh = jnp.pad(shifts.astype(F32), ((0, 0), (0, LANE - shifts.shape[1])))]
    pad x1 -> x0, local copies, waits for them, and re-layouts: 0.6 us -> none  [local(): sh = jnp.pad(shifts.astype(F32), ((0, 0), (0, LANE - shifts.shape[1])))]
where the time goes in v2:
time: 39.7 us; the launch traced here: 39.5 us
  Pallas kernels  38.9 us (98%)
  between operations  0.64 us (2%)
    pallas_call x1, Pallas kernels, local(): pl.pallas_call(functools.partial(kernel, (W, S, nl, L, NTL, R)), out_shap...  37.4 us
    pallas_call x1, Pallas kernels, local(): pl.pallas_call(unfold, out_shape=(jax.ShapeDtypeStruct((1, 3 * coeffs), F...  1.52 us

profile of v2, /device:TPU:0, one launch (start us, length us, event | category | flops | bytes accessed | tf_op | source)
XLA Modules:
  0.0 39.5 jit_solution(17827453360716239707)
XLA Ops:
  0.6 37.4 %shard_map.77 = (f32[3,4224]{1,0:T(4,128)}, f32[1,64]{1,0:T(1,128)}) custom-call(bf16[64,8448]{1,0:T(8,128)(2,1)} %x_hbm.1, s32[1,64]{1,0:T(1,128)} %bitcast.4, f32[1,4224]{1,0:T(1,128)} %ctf_ref.1, bf16[1,8448]{1,0:T(2,128)(2,1)} %proj_ref.1, f32[4224]{0:T(1024)} %noise_ref.1, s32[2,32]{1,0:T(2,128)} %bitcast.3), custom_call_target="tpu_custom_call" | custom-call | tf_op jit(solution)/shard_map/pallas_call | solution.py:406
  38.0 1.5 %shard_map.78 = (f32[1,12672]{1,0:T(1,128)}, f32[1,64]{1,0:T(1,128)}) custom-call(f32[3,4224]{1,0:T(4,128)} %get-tuple-element.6.rows_ref, f32[1,64]{1,0:T(1,128)} %get-tuple-element.7.ev_in), custom_call_target="tpu_custom_call" | custom-call | tf_op jit(solution)/shard_map/pallas_call | solution.py:453

commit v3 on v2

--- a/solution.py
+++ b/solution.py
@@ -26,7 +26,7 @@
 def kernel(
     cfg, x_hbm, gid_ref, ctf_ref, proj_ref, noise_ref, sh_ref,
     out_ref, ev_ref,
-    xbuf, cbuf, pbuf, shbuf, prow, nbuf, cos_t, sin_t, wgt, fil, wsq, pf, power, selfc,
+    xbuf, cbuf, pbuf, shbuf, prow, nbuf, cos_t, sin_t, wgt, fil, wsq, pf, power, selfc, selfr, selft, rowbuf,
     sc, scr, tot, wts, wsum, part, r1, r2, fin, fbuf,
     x_sem, own_sem, ag_ssem, ag_rsem, rl_ssem, sh_ssem, sh_rsem,
     sc_ssem, sc_rsem, r1_ssem, r1_rsem, r2_ssem, r2_rsem, f_ssem, f_rsem,
@@ -75,24 +75,24 @@
     for c in own + x_copies:
         c.start()
 
+    bar = pltpu.get_barrier_semaphore()
+    pl.semaphore_signal(bar, inc=1, device_id=(mate, s), device_id_type=MESH)
+
+    def greet(k, carry):
+        pl.semaphore_signal(
+            bar, inc=1, device_id=(chip_at(k) * 2 + core, s), device_id_type=MESH
+        )
+        return carry
+
+    lax.fori_loop(1, NC, greet, 0)
+    for d in range(1, S):
+        pl.semaphore_signal(
+            bar, inc=1, device_id=(w, lax.rem(s + d, S)), device_id_type=MESH
+        )
     own[1].wait()
     for h in range(2):
         pbuf[w, h : h + 1, :] = prow[:, pl.ds(pl.multiple_of(start + h * full, LANE), C)]
 
-    bar = pltpu.get_barrier_semaphore()
-    pl.semaphore_signal(bar, inc=1, device_id=(mate, s), device_id_type=MESH)
-
-    def greet(k, carry):
-        pl.semaphore_signal(
-            bar, inc=1, device_id=(chip_at(k) * 2 + core, s), device_id_type=MESH
-        )
-        return carry
-
-    lax.fori_loop(1, NC, greet, 0)
-    for d in range(1, S):
-        pl.semaphore_signal(
-            bar, inc=1, device_id=(w, lax.rem(s + d, S)), device_id_type=MESH
-        )
     pl.semaphore_wait(bar, NC + S - 1)
 
     def ag_pair(k, to):
@@ -181,22 +181,14 @@
         re, im = pl.ds(2 * l * LANE, LANE), pl.ds((2 * l + 1) * LANE, LANE)
         wgt[:, re] = (gain * x_re).astype(BF16)
         wgt[:, im] = (gain * x_im).astype(BF16)
-        fil[:, re] = (row * x_re).astype(BF16)
-        fil[:, im] = (row * x_im).astype(BF16)
-        here = jnp.where(first + l >= s * L, 0.5, 0.0)
-        wsq[:, cols] = curves * curves * noise * here
+        rowbuf[:, cols] = row
 
     def widen(o, carry):
         p = pbuf[o].astype(F32)
         pf[o] = p
-        power[pl.ds(o, 1), :] = jnp.sum(p * p, axis=0, keepdims=True)
         return carry
 
     lax.fori_loop(0, W, widen, 0)
-    self_g = dot(power[...], wsq[...], NT_DIMS, HIGH)
-    self_i = dot(self_g, pick, NN_DIMS, HIGH)
-    selfc[...] = jnp.concatenate([self_i[:H], self_i[H:]], axis=1)
-
     def sc_copy(b, d):
         rows = pl.ds(pl.multiple_of(b * RB, RB), RB)
         return remote(
@@ -224,14 +216,47 @@
             rot = jnp.concatenate(rots, axis=0)
             acc = acc + dot(rot, wgt[:, pl.ds(2 * l * LANE, 2 * LANE)], NT_DIMS)
         both = jnp.concatenate([acc[:RB], acc[RB:]], axis=1)
-        for q in range(QB):
-            rows = pl.ds(pl.multiple_of(b * RB + q * NT, NT), NT)
-            sc[rows, :] = both[q * NT : (q + 1) * NT] - selfc[pl.ds(b * QB + q, 1), :]
+        sc[pl.ds(pl.multiple_of(b * RB, RB), RB), :] = both
         for d in range(1, S):
             sc_copy(b, d).start()
         return carry
 
     lax.fori_loop(0, NB, score_block, 0)
+
+    def square(o, carry):
+        p = pf[o]
+        power[pl.ds(o, 1), :] = jnp.sum(p * p, axis=0, keepdims=True)
+        return carry
+
+    lax.fori_loop(0, W, square, 0)
+    for l in range(L):
+        cols = pl.ds(l * LANE, LANE)
+        curves = cbuf[:, 0, cols]
+        noise = nbuf[:, pl.ds(pl.multiple_of(start + l * LANE, LANE), LANE)]
+        here = jnp.where(first + l >= s * L, 0.5, 0.0)
+        wsq[:, cols] = curves * curves * noise * here
+    self_g = dot(power[...], wsq[...], NT_DIMS, HIGH)
+    self_i = dot(self_g, pick, NN_DIMS, HIGH)
+    selfc[...] = jnp.concatenate([self_i[:H], self_i[H:]], axis=1)
+
+    def self_copy(d):
+        return remote(
+            selfc, selfr.at[d - 1], sc_ssem.at[d - 1, NB], sc_rsem.at[d - 1, NB],
+            shift=lax.rem(s + d, S),
+        )
+
+    for d in range(1, S):
+        self_copy(d).start()
+    for l in range(L):
+        cols = pl.ds(l * LANE, LANE)
+        row = rowbuf[:, cols]
+        fil[:, pl.ds(2 * l * LANE, LANE)] = (row * xbuf[0, :, cols].astype(F32)).astype(BF16)
+        fil[:, pl.ds((2 * l + 1) * LANE, LANE)] = (row * xbuf[1, :, cols].astype(F32)).astype(BF16)
+    self_all = selfc[...]
+    for d in range(1, S):
+        self_copy(d).wait_recv()
+        self_all = self_all + selfr[d - 1]
+    selft[...] = self_all
 
     def swap(v):
         return pltpu.roll(v, R, 1)
@@ -242,8 +267,11 @@
         for d in range(1, S):
             sc_copy(b, d).wait_recv()
             v = v + scr[d - 1, rows, :]
-        tot[rows, :] = v
-        return jnp.maximum(m, jnp.max(v.reshape(RB // 8, 8, 2 * R), axis=0))
+        for q in range(QB):
+            u = v[q * NT : (q + 1) * NT] - selft[pl.ds(b * QB + q, 1), :]
+            tot[pl.ds(pl.multiple_of(b * RB + q * NT, NT), NT), :] = u
+            m = jnp.maximum(m, jnp.max(u.reshape(NT // 8, 8, 2 * R), axis=0))
+        return m
 
     m8 = lax.fori_loop(0, NB, join, jnp.full((8, 2 * R), -jnp.inf, F32))
     top = jnp.max(m8, axis=0, keepdims=True)
@@ -378,6 +406,7 @@
     lax.fori_loop(0, NB, drain_sc, 0)
     for d in range(1, S):
         f_copy(d).wait_send()
+        self_copy(d).wait_send()
 
 
 def unfold(rows_ref, ev_in, out_ref, ev_ref):
@@ -426,6 +455,9 @@
             V((W, 2, C), F32),
             V((W, C), F32),
             V((H, 2 * R), F32),
+            V((max(S - 1, 1), H, 2 * R), F32),
+            V((H, 2 * R), F32),
+            V((R, C), F32),
             V((rows, 2 * R), F32),
             V((max(S - 1, 1), rows, 2 * R), F32),
             V((rows, 2 * R), F32),
@@ -439,7 +471,7 @@
             dma((2,)), dma((4,)),
             dma((2, W // 2)), dma((2, W)), dma((2, W)),
             dma((S,)), dma((S,)),
-            dma((S, NB)), dma((S, NB)),
+            dma((S, NB + 1)), dma((S, NB + 1)),
             dma((W // 2,)), dma((W // 2,)),
             dma((W // 2,)), dma((W // 2,)),
             dma((S,)), dma((S,)),

time: 39.7 us -> 38 us (0.957)
  Pallas kernels: 38.9 us -> 37.1 us
    pallas_call x1, Pallas kernels: 37.4 us -> 35.6 us  [local(): pl.pallas_call(functools.partial(kernel, (W, S, nl, L, NTL, R)), out_shap...]
where the time goes in v3:
time: 38 us; the launch traced here: 37.8 us
  Pallas kernels  37.1 us (98%)
  between operations  0.64 us (2%)
    pallas_call x1, Pallas kernels, local(): pl.pallas_call(functools.partial(kernel, (W, S, nl, L, NTL, R)), out_shap...  35.6 us
    pallas_call x1, Pallas kernels, local(): pl.pallas_call(unfold, out_shape=(jax.ShapeDtypeStruct((1, 3 * coeffs), F...  1.52 us

profile of v3, /device:TPU:0, one launch (start us, length us, event | category | flops | bytes accessed | tf_op | source)
XLA Modules:
  0.0 37.8 jit_solution(9795449492569172573)
XLA Ops:
  0.6 35.6 %shard_map.77 = (f32[3,4224]{1,0:T(4,128)}, f32[1,64]{1,0:T(1,128)}) custom-call(bf16[64,8448]{1,0:T(8,128)(2,1)} %x_hbm.1, s32[1,64]{1,0:T(1,128)} %bitcast.4, f32[1,4224]{1,0:T(1,128)} %ctf_ref.1, bf16[1,8448]{1,0:T(2,128)(2,1)} %proj_ref.1, f32[4224]{0:T(1024)} %noise_ref.1, s32[2,32]{1,0:T(2,128)} %bitcast.3), custom_call_target="tpu_custom_call" | custom-call | tf_op jit(solution)/shard_map/pallas_call | solution.py:435
  36.3 1.5 %shard_map.78 = (f32[1,12672]{1,0:T(1,128)}, f32[1,64]{1,0:T(1,128)}) custom-call(f32[3,4224]{1,0:T(4,128)} %get-tuple-element.6.rows_ref, f32[1,64]{1,0:T(1,128)} %get-tuple-element.7.ev_in), custom_call_target="tpu_custom_call" | custom-call | tf_op jit(solution)/shard_map/pallas_call | solution.py:485

commit v4 on v3

--- a/solution.py
+++ b/solution.py
@@ -26,7 +26,7 @@
 def kernel(
     cfg, x_hbm, gid_ref, ctf_ref, proj_ref, noise_ref, sh_ref,
     out_ref, ev_ref,
-    xbuf, cbuf, pbuf, shbuf, prow, nbuf, cos_t, sin_t, wgt, fil, wsq, pf, power, selfc, selfr, selft, rowbuf,
+    xbuf, cbuf, pbuf, shbuf, prow, nbuf, cos_t, sin_t, wgt, fil, wsq, power, selfc, selfr, selft, rowbuf,
     sc, scr, tot, wts, wsum, part, r1, r2, fin, fbuf,
     x_sem, own_sem, ag_ssem, ag_rsem, rl_ssem, sh_ssem, sh_rsem,
     sc_ssem, sc_rsem, r1_ssem, r1_rsem, r2_ssem, r2_rsem, f_ssem, f_rsem,
@@ -183,12 +183,6 @@
         wgt[:, im] = (gain * x_im).astype(BF16)
         rowbuf[:, cols] = row
 
-    def widen(o, carry):
-        p = pbuf[o].astype(F32)
-        pf[o] = p
-        return carry
-
-    lax.fori_loop(0, W, widen, 0)
     def sc_copy(b, d):
         rows = pl.ds(pl.multiple_of(b * RB, RB), RB)
         return remote(
@@ -205,8 +199,8 @@
             for h in range(2):
                 for q in range(QB):
                     o = h * H + b * QB + q
-                    pr = pf[o, 0:1, cols]
-                    pi = pf[o, 1:2, cols]
+                    pair = pbuf[o, :, cols].astype(F32)
+                    pr, pi = pair[0:1], pair[1:2]
                     rots.append(
                         jnp.concatenate(
                             [(pr * ct + pi * st).astype(BF16), (pi * ct - pr * st).astype(BF16)],
@@ -224,7 +218,7 @@
     lax.fori_loop(0, NB, score_block, 0)
 
     def square(o, carry):
-        p = pf[o]
+        p = pbuf[o].astype(F32)
         power[pl.ds(o, 1), :] = jnp.sum(p * p, axis=0, keepdims=True)
         return carry
 
@@ -452,7 +446,6 @@
             V((R, 2 * C), BF16),
             V((R, 2 * C), BF16),
             V((W, C), F32),
-            V((W, 2, C), F32),
             V((W, C), F32),
             V((H, 2 * R), F32),
             V((max(S - 1, 1), H, 2 * R), F32),

time: 38 us -> 37.9 us (level)
  no operation moved by 1% of the time
where the time goes in v4:
time: 37.9 us; the launch traced here: 37.7 us
  Pallas kernels  37.1 us (98%)
  between operations  0.64 us (2%)
    pallas_call x1, Pallas kernels, local(): pl.pallas_call(functools.partial(kernel, (W, S, nl, L, NTL, R)), out_shap...  35.5 us
    pallas_call x1, Pallas kernels, local(): pl.pallas_call(unfold, out_shape=(jax.ShapeDtypeStruct((1, 3 * coeffs), F...  1.52 us

profile of v4, /device:TPU:0, one launch (start us, length us, event | category | flops | bytes accessed | tf_op | source)
XLA Modules:
  0.0 37.7 jit_solution(15703677593985618559)
XLA Ops:
  0.6 35.5 %shard_map.77 = (f32[3,4224]{1,0:T(4,128)}, f32[1,64]{1,0:T(1,128)}) custom-call(bf16[64,8448]{1,0:T(8,128)(2,1)} %x_hbm.1, s32[1,64]{1,0:T(1,128)} %bitcast.4, f32[1,4224]{1,0:T(1,128)} %ctf_ref.1, bf16[1,8448]{1,0:T(2,128)(2,1)} %proj_ref.1, f32[4224]{0:T(1024)} %noise_ref.1, s32[2,32]{1,0:T(2,128)} %bitcast.3), custom_call_target="tpu_custom_call" | custom-call | tf_op jit(solution)/shard_map/pallas_call | solution.py:429
  36.2 1.5 %shard_map.78 = (f32[1,12672]{1,0:T(1,128)}, f32[1,64]{1,0:T(1,128)}) custom-call(f32[3,4224]{1,0:T(4,128)} %get-tuple-element.6.rows_ref, f32[1,64]{1,0:T(1,128)} %get-tuple-element.7.ev_in), custom_call_target="tpu_custom_call" | custom-call | tf_op jit(solution)/shard_map/pallas_call | solution.py:478
